TPU v7x, 512 devices: a whole 4x8x8 slice. The times are simulated.
512 devices in a mesh: segment: 8 (over x, core), adapter: 64 (over z, y).
Axes of the slice: x: 4, y: 8, z: 8, core: 2. Of those that a mesh axis runs over, the one named last changes fastest.
Arguments:
- incoming: bfloat16 [4096, 8192], P(('segment', 'adapter')), may hold values from -6 to 6
- attention_norm_gain: float32 [8, 8192], P('segment'), may hold values from 0.1 to 1.9
- query_weight: bfloat16 [8, 8192, 8192], P('segment', None, 'adapter'), may hold values from -0.0625 to 0.0625
- adapter_down_weight: bfloat16 [8, 64, 8192, 64], P('segment', 'adapter'), may hold values from -0.0625 to 0.0625
- adapter_up_weight: bfloat16 [8, 64, 64, 8192], P('segment', None, None, 'adapter'), may hold values from -0.75 to 0.75
- request_adapter_index: int32 [4096], P('segment'), may hold values from 0 to 63, as said below
- cache_valid_length: int32 [4096], P('segment'), may hold values from 1 to 16
- key_value_cache: bfloat16 [4096, 2, 16, 1024], P(('segment', 'adapter')), may hold values from -1500 to 1500, as said below
Outputs:
- context: bfloat16 [4096, 8192], P(('segment', 'adapter'))
Inputs may be any that keep to these rules, and one draw needn't show every extreme that they name: `request_adapter_index`: adapter a is owned by index a // 1 of adapter. At most 32 of the 512 requests of one section name adapters of one owner, and in every section some owner has exactly 32. `key_value_cache`: positions at or after a request's length hold unused entries.
All inputs are finite; a program needn't handle non-finite values.
Results may differ from a plain program's by a relative error of at most 0.04.
Values may be sent and summed in bfloat16 or wider, within the bound.
No kernel may reach another device: no remote copies, remote signals or barrier semaphores. Data moves between devices by JAX's collectives and lax.ppermute only.
A program may use at most 64 MiB of HBM per device.

v0:
```python
import jax
import jax.numpy as jnp
from jax import lax
from jax.sharding import PartitionSpec as P

MODEL_WIDTH = 8192
HEADS = 64
KVH = 8
HD = 128
CTX = 16
adapter_scale = 0.5
norm_eps = 1e-05


def from_behind(value, axis, by):
    devices = lax.axis_size(axis)
    return lax.ppermute(value, axis, [(i, (i + by) % devices) for i in range(devices)])


def body(
    incoming,
    attention_norm_gain,
    query_weight,
    adapter_down_weight,
    adapter_up_weight,
    request_adapter_index,
    cache_valid_length,
    key_value_cache,
):
    received_rows = from_behind(incoming, "segment", 1)
    values = received_rows.astype(jnp.float32)
    mean_square = jnp.mean(values * values, axis=-1, keepdims=True)
    normalized_input = (values * lax.rsqrt(mean_square + norm_eps) * attention_norm_gain[0]).astype(
        jnp.bfloat16
    )
    tok_dev = received_rows.shape[0]
    position = lax.axis_index("adapter")
    segment_rows = request_adapter_index.shape[0]
    weight = query_weight[0]
    column_list = weight.shape[1]
    down_matrices = adapter_down_weight[0]
    ad_dev = down_matrices.shape[0]
    adapter_rank_width = down_matrices.shape[2]
    adapter_bank = adapter_up_weight.shape[1]
    owner_of = request_adapter_index // ad_dev
    local_of = request_adapter_index % ad_dev
    row_piece = lax.all_gather(normalized_input, "adapter", axis=0, tiled=True)
    plain = jnp.dot(row_piece, weight, preferred_element_type=jnp.float32)
    shrunk = jnp.einsum("td,adr->tar", row_piece, down_matrices, preferred_element_type=jnp.float32)
    projected = jnp.concatenate(
        [plain, shrunk.reshape(row_piece.shape[0], ad_dev * adapter_rank_width)], axis=1
    )
    base_query = projected[:, :column_list]
    shrunk_all = projected[:, column_list:].reshape(segment_rows, ad_dev, adapter_rank_width)
    select_mask = (local_of[:, None] == jnp.arange(ad_dev, dtype=jnp.int32)[None, :]) & (
        owner_of == position
    )[:, None]
    shrunk_mine = jnp.sum(shrunk_all * select_mask[:, :, None].astype(jnp.float32), axis=1)
    shrunk_tok = lax.psum(shrunk_mine, "adapter").astype(jnp.bfloat16)
    adapter_hot = (
        request_adapter_index[:, None] == jnp.arange(adapter_bank, dtype=jnp.int32)[None, :]
    ).astype(jnp.bfloat16)
    spread = (adapter_hot[:, :, None] * shrunk_tok[:, None, :]).reshape(
        segment_rows, adapter_bank * adapter_rank_width
    )
    adapter_update = jnp.dot(
        spread,
        adapter_up_weight[0].reshape(adapter_bank * adapter_rank_width, column_list),
        preferred_element_type=jnp.float32,
    )
    query_rows = (base_query + adapter_scale * adapter_update).astype(jnp.bfloat16)
    own_queries = lax.all_to_all(query_rows, "adapter", split_axis=0, concat_axis=1, tiled=True)
    own_lengths = lax.dynamic_slice_in_dim(cache_valid_length, position * tok_dev, tok_dev)
    group_size = HEADS // KVH
    query_heads = own_queries.reshape(tok_dev, KVH, group_size, HD)
    cached_keys = key_value_cache[:, 0].reshape(tok_dev, CTX, KVH, HD)
    cached_values = key_value_cache[:, 1].reshape(tok_dev, CTX, KVH, HD)
    scores = jnp.einsum(
        "tkgd,tckd->tkgc", query_heads, cached_keys, preferred_element_type=jnp.float32
    ) * HD ** (-0.5)
    is_live = jnp.arange(CTX, dtype=jnp.int32)[None, :] < own_lengths[:, None]
    scores = jnp.where(is_live[:, None, None, :], scores, -jnp.inf)
    row_max = jnp.max(scores, axis=-1, keepdims=True)
    expsum = jnp.exp(scores - row_max)
    probs = (expsum / jnp.sum(expsum, axis=-1, keepdims=True)).astype(jnp.bfloat16)
    context = jnp.einsum(
        "tkgc,tckd->tkgd", probs, cached_values, preferred_element_type=jnp.float32
    )
    return context.astype(jnp.bfloat16).reshape(tok_dev, MODEL_WIDTH)


def solution(mesh):
    in_specs = (
        P(("segment", "adapter"), None),
        P("segment", None),
        P("segment", None, "adapter"),
        P("segment", "adapter", None, None),
        P("segment", None, None, "adapter"),
        P("segment"),
        P("segment"),
        P(("segment", "adapter"), None, None, None),
    )
    out_specs = P(("segment", "adapter"), None)
    return jax.shard_map(body, mesh=mesh, in_specs=in_specs, out_specs=out_specs, check_vma=False)
```

profile of v0, /device:TPU:2, one launch (start us, length us, event | category | flops | bytes accessed | tf_op | source)
XLA Modules:
  0.0 437.0 jit_solution(6237502555371092495)
XLA Ops:
  6.5 0.0 all-gather.2.cloned.1.call-start
  6.5 0.0 collective-permute-start
  6.5 4.6 %collective-permute-done = bf16[8,8192]{1,0:T(8,128)(2,1)S(1)} collective-permute-done((bf16[8,8192]{1,0:T(8,128)(2,1)}, bf16[8,8192]{1,0:T(8,128)(2,1)S(1)}, u32[]{:S(2)}, u32[]{:S(2)}) %collective-permute-start) | collective-permute-done | bytes 131104 | tf_op jit(solution)/shard_map/ppermute | solution.py:17
  11.1 0.2 fusion.11
  11.3 1.5 fusion.13
  12.8 0.0 all-gather.2.cloned.1.call-update
  12.9 0.7 compare_convert_fusion
  13.6 0.7 fusion.19
  14.3 102.8 %all-gather.2.cloned.1.call-done = bf16[512,8192]{1,0:T(8,128)(2,1)} async-done(((bf16[8,8192]{1,0:T(8,128)(2,1)}), bf16[512,8192]{1,0:T(8,128)(2,1)}) %all-gather.2.cloned.1.call-update) | async-done | bytes 8388624 | tf_op jit(solution)/shard_map/all_gather | solution.py:47
  117.0 6.3 %convolution_multiply_fusion.2 = f32[512,64]{0,1:T(8,128)S(1)} fusion(bf16[512,8192]{1,0:T(8,128)(2,1)} %all-gather.2.cloned.1.call-done, bf16[1,1,8192,64]{2,3,1,0:T(8,128)(2,1)} %param.11, f32[512]{0:T(512)S(1)} %compare_convert_fusion), kind=kOutput, calls=%fused_computation.14 | convolution fusion | flops 536903680 | bytes 9570304 | tf_op jit(solution)/shard_map/td,adr->tar/dot_general | solution.py:49
  123.3 277.7 %all-reduce.1 = bf16[512,64]{0,1:T(8,128)(2,1)S(1)} all-reduce(f32[512,64]{0,1:T(8,128)S(1)} %convolution_multiply_fusion.2), channel_id=1, replica_groups=mesh['segment'=8,'adapter'=64] {'adapter'}, use_global_device_ids=true, to_apply=%region_1.2 | all-reduce | flops 32768 | bytes 196608 | tf_op jit(solution)/shard_map/psum | solution.py:59
  401.0 0.3 broadcast_multiply_fusion
  401.3 0.0 copy-start.1
  401.3 5.8 %fusion.1 = f32[512,128]{1,0:T(8,128)S(1)} fusion(bf16[512,8192]{1,0:T(8,128)(2,1)} %all-gather.2.cloned.1.call-done, bf16[1,8192,128]{2,1,0:T(8,128)(2,1)S(1)} %copy-done), kind=kOutput, calls=%fused_computation.1 | convolution fusion | flops 1073741824 | bytes 10747904 | tf_op jit(solution)/shard_map/dot_general | solution.py:48
  407.1 0.0 copy-start.2
  407.1 2.0 fusion.9
  409.1 6.2 %all-to-all-start = ((bf16[64,8,128]{2,1,0:T(8,128)(2,1)}), bf16[64,8,128]{2,1,0:T(8,128)(2,1)S(1)}, u32[]{:S(2)}, u32[]{:S(2)}) async-start(bf16[64,8,128]{2,1,0:T(8,128)(2,1)} %fusion.9), calls=%async_computation | async-start | bytes 262144 | tf_op jit(solution)/shard_map/all_to_all | solution.py:72
  415.5 0.8 dynamic_slice.3
  416.2 0.1 iota_compare_fusion.1
  416.3 11.7 %all-to-all-done = bf16[64,8,128]{2,1,0:T(8,128)(2,1)S(1)} async-done(((bf16[64,8,128]{2,1,0:T(8,128)(2,1)}), bf16[64,8,128]{2,1,0:T(8,128)(2,1)S(1)}, u32[]{:S(2)}, u32[]{:S(2)}) %all-to-all-start) | async-done | bytes 131104 | tf_op jit(solution)/shard_map/all_to_all | solution.py:72
  428.0 0.3 fusion.4
  428.2 0.2 fusion.21
  428.5 1.0 fusion.8
  429.5 0.7 copy.26
  (8 shorter events, 0.1 us)
Async XLA Ops:
  6.5 394.7 %copy-start = (bf16[1,8192,128]{2,1,0:T(8,128)(2,1)S(1)}, bf16[1,8192,128]{2,1,0:T(8,128)(2,1)}, u32[]{:S(2)}) copy-start(bf16[1,8192,128]{2,1,0:T(8,128)(2,1)} %param.10) | copy-start | bytes 6291460
  6.5 110.5 %all-gather.2.cloned.1.call-start = ((), (), s32[]{:S(2)}) async-start(), calls=%async_computation.1 | async-start | bytes 8519680 | tf_op jit(solution)/shard_map/all_gather | solution.py:47
  6.5 4.6 %collective-permute-start = (bf16[8,8192]{1,0:T(8,128)(2,1)}, bf16[8,8192]{1,0:T(8,128)(2,1)S(1)}, u32[]{:S(2)}, u32[]{:S(2)}) collective-permute-start(bf16[8,8192]{1,0:T(8,128)(2,1)} %param.8), channel_id=1, source_target_pairs={{0,64},{64,128},{128,192},{192,256},{256,320},{320,384},{384,448},... | collective-permute-start | bytes 393224 | tf_op jit(solution)/shard_map/ppermute | solution.py:17
  401.3 5.8 %copy-start.1 = (bf16[1,64,64,128]{3,2,1,0:T(8,128)(2,1)S(1)}, bf16[1,64,64,128]{3,2,1,0:T(8,128)(2,1)}, u32[]{:S(2)}) copy-start(bf16[1,64,64,128]{3,2,1,0:T(8,128)(2,1)} %param.12) | copy-start | bytes 3145732
  407.1 8.2 %copy-start.2 = (bf16[8,2,16,1024]{3,2,1,0:T(8,128)(2,1)S(1)}, bf16[8,2,16,1024]{3,2,1,0:T(8,128)(2,1)}, u32[]{:S(2)}) copy-start(bf16[8,2,16,1024]{3,2,1,0:T(8,128)(2,1)} %param.15) | copy-start | bytes 1572868
  409.1 18.9 %all-to-all-start = ((bf16[64,8,128]{2,1,0:T(8,128)(2,1)}), bf16[64,8,128]{2,1,0:T(8,128)(2,1)S(1)}, u32[]{:S(2)}, u32[]{:S(2)}) async-start(bf16[64,8,128]{2,1,0:T(8,128)(2,1)} %fusion.9), calls=%async_computation | async-start | bytes 262144 | tf_op jit(solution)/shard_map/all_to_all | solution.py:72
Sparse Core Ops, SparseCore 0:
  13.0 103.9 all-gather.1
where the time goes:
time: 437 us
  blocking collectives  278 us (64%)
  waiting for transfers between devices  119 us (27%)
  matrix products  15.3 us (4%)
  between operations  13.5 us (3%)
  starting transfers between devices  6.2 us (1%)
    psum x1, blocking collectives, body(): shrunk_tok = lax.psum(shrunk_mine, 'adapter').astype(jnp.bfloat16)  278 us
    all_gather x1, waiting for transfers between devices, body(): row_piece = lax.all_gather(normalized_input, 'adapter', axis=0, tiled=True)  103 us
    all_to_all x1, waiting for transfers between devices, body(): lax.all_to_all(query_rows, 'adapter', split_axis=0, concat_axis=1, tiled=...  11.7 us
  transfers between devices with their start and end apart: 3, of which 3 were waited for; matrix products, arithmetic and copies ran while one was open for 1% of the time, Pallas kernels for 0%

commit v1 on v0

--- a/solution.py
+++ b/solution.py
@@ -10,6 +10,12 @@
 CTX = 16
 adapter_scale = 0.5
 norm_eps = 1e-05
+
+
+def gather_by_exchange(x, axis, dim):
+    size = lax.axis_size(axis)
+    repeats = [size if d == dim else 1 for d in range(x.ndim)]
+    return lax.all_to_all(jnp.tile(x, repeats), axis, split_axis=dim, concat_axis=dim, tiled=True)
 
 
 def from_behind(value, axis, by):
@@ -44,7 +50,7 @@
     adapter_bank = adapter_up_weight.shape[1]
     owner_of = request_adapter_index // ad_dev
     local_of = request_adapter_index % ad_dev
-    row_piece = lax.all_gather(normalized_input, "adapter", axis=0, tiled=True)
+    row_piece = gather_by_exchange(normalized_input, "adapter", 0)
     plain = jnp.dot(row_piece, weight, preferred_element_type=jnp.float32)
     shrunk = jnp.einsum("td,adr->tar", row_piece, down_matrices, preferred_element_type=jnp.float32)
     projected = jnp.concatenate(

time: 437 us -> 622 us (1.42)
  the two profiles are of different devices: /device:TPU:2 before, /device:TPU:6 now
where the time goes in v1:
time: 622 us
  blocking collectives  326 us (52%)
  waiting for transfers between devices  249 us (40%)
  starting transfers between devices  23.8 us (4%)
  matrix products  15 us (2%)
    psum x1, blocking collectives, body(): shrunk_tok = lax.psum(shrunk_mine, 'adapter').astype(jnp.bfloat16)  326 us
    all_to_all x1, waiting for transfers between devices, gather_by_exchange(): lax.all_to_all(jnp.tile(x, repeats), axis, split_axis=dim, concat_axis=di...  233 us
    all_to_all x1, starting transfers between devices, gather_by_exchange(): lax.all_to_all(jnp.tile(x, repeats), axis, split_axis=dim, concat_axis=di...  17 us
  transfers between devices with their start and end apart: 3, of which 3 were waited for; matrix products, arithmetic and copies ran while one was open for 0% of the time, Pallas kernels for 0%

profile of v1, /device:TPU:6, one launch (start us, length us, event | category | flops | bytes accessed | tf_op | source)
XLA Modules:
  0.0 622.0 jit_solution(16064373959628131548)
XLA Ops:
  0.0 0.0 copy-start
  0.0 0.0 collective-permute-start
  0.0 4.6 collective-permute-done
  4.6 0.2 fusion.17
  4.8 0.9 fusion.19
  5.7 4.2 tile.2
  9.9 17.0 %all-to-all-start = ((bf16[64,8,8192]{2,1,0:T(8,128)(2,1)}), bf16[64,8,8192]{2,1,0:T(8,128)(2,1)}, u32[]{:S(2)}, u32[]{:S(2)}) async-start(bf16[64,8,8192]{2,1,0:T(8,128)(2,1)} %tile.2), calls=%async_computation | async-start | bytes 16777216 | tf_op jit(solution)/shard_map/all_to_all | solution.py:18
  26.9 233.1 %all-to-all-done = bf16[64,8,8192]{2,1,0:T(8,128)(2,1)} async-done(((bf16[64,8,8192]{2,1,0:T(8,128)(2,1)}), bf16[64,8,8192]{2,1,0:T(8,128)(2,1)}, u32[]{:S(2)}, u32[]{:S(2)}) %all-to-all-start) | async-done | bytes 8388640 | tf_op jit(solution)/shard_map/all_to_all | solution.py:18
  260.0 0.0 copy-done.2
  260.0 6.0 fusion.13
  266.1 326.1 %all-reduce.1 = bf16[512,64]{0,1:T(8,128)(2,1)S(1)} all-reduce(f32[512,64]{0,1:T(8,128)S(1)} %fusion.13), channel_id=1, replica_groups=mesh['segment'=8,'adapter'=64] {'adapter'}, use_global_device_ids=true, to_apply=%region_1.2 | all-reduce | flops 32768 | bytes 196608 | tf_op jit(solution)/shard_map/psum | solution.py:65
  592.2 0.3 broadcast_multiply_fusion
  592.5 0.0 copy-start.1
  592.5 5.8 fusion.3
  598.3 0.0 copy-start.3
  598.3 2.0 fusion.12
  600.3 6.8 %all-to-all-start.1 = ((bf16[64,8,128]{2,1,0:T(8,128)(2,1)}), bf16[64,8,128]{2,1,0:T(8,128)(2,1)S(1)}, u32[]{:S(2)}, u32[]{:S(2)}) async-start(bf16[64,8,128]{2,1,0:T(8,128)(2,1)} %fusion.12), calls=%async_computation.1 | async-start | bytes 262144 | tf_op jit(solution)/shard_map/all_to_all | solution.py:78
  607.2 0.8 dynamic_slice.3
  608.0 0.1 iota_compare_fusion.1
  608.1 11.7 %all-to-all-done.1 = bf16[64,8,128]{2,1,0:T(8,128)(2,1)S(1)} async-done(((bf16[64,8,128]{2,1,0:T(8,128)(2,1)}), bf16[64,8,128]{2,1,0:T(8,128)(2,1)S(1)}, u32[]{:S(2)}, u32[]{:S(2)}) %all-to-all-start.1) | async-done | bytes 131104 | tf_op jit(solution)/shard_map/all_to_all | solution.py:78
  619.8 0.3 fusion.7
  620.0 0.2 fusion.27
  620.2 1.0 fusion.11
  621.2 0.7 copy.26
  (12 shorter events, 0.2 us)
Async XLA Ops:
  0.0 592.5 %copy-start = (bf16[1,8192,128]{2,1,0:T(8,128)(2,1)S(1)}, bf16[1,8192,128]{2,1,0:T(8,128)(2,1)}, u32[]{:S(2)}) copy-start(bf16[1,8192,128]{2,1,0:T(8,128)(2,1)} %param.10) | copy-start | bytes 6291460
  0.0 4.6 collective-permute-start
  9.9 17.0 %copy-start.4 = (s32[512]{0:T(512)S(1)}, s32[512]{0:T(512)}, u32[]{:S(2)}) copy-start(s32[512]{0:T(512)} %param.13) | copy-start | bytes 6148
  9.9 250.2 %copy-start.2 = (bf16[1,1,8192,64]{2,3,1,0:T(8,128)(2,1)S(1)}, bf16[1,1,8192,64]{2,3,1,0:T(8,128)(2,1)}, u32[]{:S(2)}) copy-start(bf16[1,1,8192,64]{2,3,1,0:T(8,128)(2,1)} %param.11) | copy-start | bytes 3145732
  9.9 250.2 %all-to-all-start = ((bf16[64,8,8192]{2,1,0:T(8,128)(2,1)}), bf16[64,8,8192]{2,1,0:T(8,128)(2,1)}, u32[]{:S(2)}, u32[]{:S(2)}) async-start(bf16[64,8,8192]{2,1,0:T(8,128)(2,1)} %tile.2), calls=%async_computation | async-start | bytes 16777216 | tf_op jit(solution)/shard_map/all_to_all | solution.py:18
  592.5 5.8 copy-start.1
  598.3 8.8 %copy-start.3 = (bf16[8,2,16,1024]{3,2,1,0:T(8,128)(2,1)S(1)}, bf16[8,2,16,1024]{3,2,1,0:T(8,128)(2,1)}, u32[]{:S(2)}) copy-start(bf16[8,2,16,1024]{3,2,1,0:T(8,128)(2,1)} %param.15) | copy-start | bytes 1572868
  600.3 19.5 %all-to-all-start.1 = ((bf16[64,8,128]{2,1,0:T(8,128)(2,1)}), bf16[64,8,128]{2,1,0:T(8,128)(2,1)S(1)}, u32[]{:S(2)}, u32[]{:S(2)}) async-start(bf16[64,8,128]{2,1,0:T(8,128)(2,1)} %fusion.12), calls=%async_computation.1 | async-start | bytes 262144 | tf_op jit(solution)/shard_map/all_to_all | solution.py:78

commit v2 on v0

--- a/solution.py
+++ b/solution.py
@@ -2,6 +2,7 @@
 import jax.numpy as jnp
 from jax import lax
 from jax.sharding import PartitionSpec as P
+from jax.lax import all_gather
 
 MODEL_WIDTH = 8192
 HEADS = 64
@@ -56,7 +57,7 @@
         owner_of == position
     )[:, None]
     shrunk_mine = jnp.sum(shrunk_all * select_mask[:, :, None].astype(jnp.float32), axis=1)
-    shrunk_tok = lax.psum(shrunk_mine, "adapter").astype(jnp.bfloat16)
+    shrunk_tok = jnp.sum(all_gather(shrunk_mine, axis_name="adapter"), 0).astype(jnp.bfloat16)
     adapter_hot = (
         request_adapter_index[:, None] == jnp.arange(adapter_bank, dtype=jnp.int32)[None, :]
     ).astype(jnp.bfloat16)

time: 437 us -> 268 us (0.61)
  blocking collectives: 278 us -> 0 us
  waiting for transfers between devices: 119 us -> 212 us
  local copies, waits for them, and re-layouts: 1.66 us -> 10.7 us
    psum x1 -> x0, blocking collectives: 278 us -> none  [body(): shrunk_tok = lax.psum(shrunk_mine, 'adapter').astype(jnp.bfloat16)]
    all_gather x0 -> x1, waiting for transfers between devices: none -> 91.8 us  [body(): all_gather(shrunk_mine, axis_name='adapter')]
    unnamed x9 -> x12, local copies, waits for them, and re-layouts: 0.86 us -> 9.89 us
  transfers between devices with their start and end apart: 3 -> 4, of which waited for: 3 -> 4; matrix products, arithmetic and copies ran while one was open for 1% -> 3% of each run, Pallas kernels for 0% -> 0%
where the time goes in v2:
time: 268 us; the launch traced here: 267 us
  waiting for transfers between devices  212 us (79%)
  matrix products  15.8 us (6%)
  between operations  13.5 us (5%)
  local copies, waits for them, and re-layouts  10.7 us (4%)
  starting transfers between devices  10.1 us (4%)
  other arithmetic  5.58 us (2%)
    all_gather x1, waiting for transfers between devices, body(): row_piece = lax.all_gather(normalized_input, 'adapter', axis=0, tiled=True)  103 us
    all_gather x1, waiting for transfers between devices, body(): all_gather(shrunk_mine, axis_name='adapter')  91.8 us
    all_to_all x1, waiting for transfers between devices, body(): lax.all_to_all(query_rows, 'adapter', split_axis=0, concat_axis=1, tiled=...  11.7 us
    all_to_all x1, starting transfers between devices, body(): lax.all_to_all(query_rows, 'adapter', split_axis=0, concat_axis=1, tiled=...  10 us
    unnamed x12, local copies, waits for them, and re-layouts  9.89 us
    dot_general x1, matrix products, body(): jnp.einsum('td,adr->tar', row_piece, down_matrices, preferred_element_typ...  6.93 us
    dot_general x1, matrix products, body(): plain = jnp.dot(row_piece, weight, preferred_element_type=jnp.float32)  5.7 us
  transfers between devices with their start and end apart: 4, of which 4 were waited for; matrix products, arithmetic and copies ran while one was open for 3% of the time, Pallas kernels for 0%

profile of v2, /device:TPU:2, one launch (start us, length us, event | category | flops | bytes accessed | tf_op | source)
XLA Modules:
  0.0 267.3 jit_solution(282248917349415748)
XLA Ops:
  6.5 4.6 %collective-permute-done = bf16[8,8192]{1,0:T(8,128)(2,1)S(1)} collective-permute-done((bf16[8,8192]{1,0:T(8,128)(2,1)}, bf16[8,8192]{1,0:T(8,128)(2,1)S(1)}, u32[]{:S(2)}, u32[]{:S(2)}) %collective-permute-start) | collective-permute-done | bytes 131104 | tf_op jit(solution)/shard_map/ppermute | solution.py:18
  11.1 0.2 fusion.11
  11.3 1.5 fusion.13
  12.8 0.0 all-gather.4.cloned.1.call-update
  12.9 0.0 all-gather.6.cloned.1.call-start
  12.9 0.7 compare_convert_fusion
  13.6 103.4 %all-gather.4.cloned.1.call-done = bf16[512,8192]{1,0:T(8,128)(2,1)} async-done(((bf16[8,8192]{1,0:T(8,128)(2,1)}), bf16[512,8192]{1,0:T(8,128)(2,1)}) %all-gather.4.cloned.1.call-update) | async-done | bytes 8388624 | tf_op jit(solution)/shard_map/all_gather | solution.py:48
  117.0 6.9 %convolution_multiply_fusion.2 = f32[512,64]{0,1:T(8,128)} fusion(bf16[512,8192]{1,0:T(8,128)(2,1)} %all-gather.4.cloned.1.call-done, bf16[1,1,8192,64]{2,3,1,0:T(8,128)(2,1)} %param.11, f32[512]{0:T(512)S(1)} %compare_convert_fusion), kind=kOutput, calls=%fused_computation.15 | convolution fusion | flops 536903680 | bytes 9570304 | tf_op jit(solution)/shard_map/td,adr->tar/dot_general | solution.py:50
  124.0 0.0 all-gather.6.cloned.1.call-update
  124.0 5.7 %fusion.1 = f32[512,128]{1,0:T(8,128)S(1)} fusion(bf16[512,8192]{1,0:T(8,128)(2,1)} %all-gather.4.cloned.1.call-done, bf16[1,8192,128]{2,1,0:T(8,128)(2,1)S(1)} %copy-done), kind=kOutput, calls=%fused_computation.2 | convolution fusion | flops 1073741824 | bytes 10747904 | tf_op jit(solution)/shard_map/dot_general | solution.py:49
  129.7 91.8 %all-gather.6.cloned.1.call-done = f32[32768,64]{0,1:T(8,128)} async-done(((f32[512,64]{0,1:T(8,128)}), f32[32768,64]{0,1:T(8,128)}) %all-gather.6.cloned.1.call-update) | async-done | bytes 8388624 | tf_op jit(solution)/shard_map/all_gather | solution.py:60
  221.6 8.1 %copy.13 = f32[8,8,64,512]{3,2,1,0:T(8,128)S(1)} copy(f32[8,8,64,512]{3,1,2,0:T(8,128)} %bitcast.43) | data formatting | bytes 16777216
  229.7 2.6 bitcast_reduce_fusion
  232.3 0.3 broadcast_multiply_fusion
  232.6 0.9 copy-done.1
  233.5 2.0 fusion.9
  235.5 10.0 %all-to-all-start = ((bf16[64,8,128]{2,1,0:T(8,128)(2,1)}), bf16[64,8,128]{2,1,0:T(8,128)(2,1)S(1)}, u32[]{:S(2)}, u32[]{:S(2)}) async-start(bf16[64,8,128]{2,1,0:T(8,128)(2,1)} %fusion.9), calls=%async_computation | async-start | bytes 262144 | tf_op jit(solution)/shard_map/all_to_all | solution.py:73
  245.7 0.8 dynamic_slice.3
  246.4 0.1 iota_compare_fusion.1
  246.5 11.7 %all-to-all-done = bf16[64,8,128]{2,1,0:T(8,128)(2,1)S(1)} async-done(((bf16[64,8,128]{2,1,0:T(8,128)(2,1)}), bf16[64,8,128]{2,1,0:T(8,128)(2,1)S(1)}, u32[]{:S(2)}, u32[]{:S(2)}) %all-to-all-start) | async-done | bytes 131104 | tf_op jit(solution)/shard_map/all_to_all | solution.py:73
  258.2 0.3 fusion.4
  258.5 0.2 fusion.21
  258.7 1.0 fusion.8
  259.7 0.7 copy.26
  (14 shorter events, 0.2 us)
Async XLA Ops:
  6.5 117.5 %copy-start = (bf16[1,8192,128]{2,1,0:T(8,128)(2,1)S(1)}, bf16[1,8192,128]{2,1,0:T(8,128)(2,1)}, u32[]{:S(2)}) copy-start(bf16[1,8192,128]{2,1,0:T(8,128)(2,1)} %param.10) | copy-start | bytes 6291460
  6.5 110.5 %all-gather.4.cloned.1.call-start = ((), (), s32[]{:S(2)}) async-start(), calls=%async_computation.1 | async-start | bytes 8519680 | tf_op jit(solution)/shard_map/all_gather | solution.py:48
  6.5 4.6 %collective-permute-start = (bf16[8,8192]{1,0:T(8,128)(2,1)}, bf16[8,8192]{1,0:T(8,128)(2,1)S(1)}, u32[]{:S(2)}, u32[]{:S(2)}) collective-permute-start(bf16[8,8192]{1,0:T(8,128)(2,1)} %param.8), channel_id=1, source_target_pairs={{0,64},{64,128},{128,192},{192,256},{256,320},{320,384},{384,448},... | collective-permute-start | bytes 393224 | tf_op jit(solution)/shard_map/ppermute | solution.py:18
  12.9 208.7 %all-gather.6.cloned.1.call-start = ((), (), s32[]{:S(2)}) async-start(), calls=%async_computation.2 | async-start | bytes 8519680 | tf_op jit(solution)/shard_map/all_gather | solution.py:60
  13.6 110.4 %copy-start.3 = (s32[512]{0:T(512)S(1)}, s32[512]{0:T(512)}, u32[]{:S(2)}) copy-start(s32[512]{0:T(512)} %param.13) | copy-start | bytes 6148
  232.3 1.2 copy-start.1
  232.3 13.2 %copy-start.2 = (bf16[8,2,16,1024]{3,2,1,0:T(8,128)(2,1)S(1)}, bf16[8,2,16,1024]{3,2,1,0:T(8,128)(2,1)}, u32[]{:S(2)}) copy-start(bf16[8,2,16,1024]{3,2,1,0:T(8,128)(2,1)} %param.15) | copy-start | bytes 1572868
  235.5 22.8 %all-to-all-start = ((bf16[64,8,128]{2,1,0:T(8,128)(2,1)}), bf16[64,8,128]{2,1,0:T(8,128)(2,1)S(1)}, u32[]{:S(2)}, u32[]{:S(2)}) async-start(bf16[64,8,128]{2,1,0:T(8,128)(2,1)} %fusion.9), calls=%async_computation | async-start | bytes 262144 | tf_op jit(solution)/shard_map/all_to_all | solution.py:73
Sparse Core Ops, SparseCore 0:
  13.0 103.9 all-gather.3
  124.1 97.4 all-gather.5
